TPU v7x, 32 devices: a whole 2x2x4 slice. The times are simulated.
32 devices in a mesh: tp: 4 (over y, core), ad: 8 (over z, x).
Axes of the slice: x: 2, y: 2, z: 4, core: 2. Of those that a mesh axis runs over, the one named last changes fastest.
Arguments:
- hidden: bfloat16 [2048, 8192], P('ad'), may hold values from -6 to 6
- key_value_weight: bfloat16 [8192, 2048], P(None, 'tp'), may hold values from -0.0625 to 0.0625
- request_group: int32 [2048, 1], P('ad'), may hold values from 0 to 7; in each aligned block of 256 rows (0 to 255, 256 to 511, ...) at most 64 rows name the same one
- request_member: int32 [2048], P('ad'), may hold values from 0 to 3
- adapter_down_weight: bfloat16 [8192, 2048], P('tp', 'ad'), may hold values from -0.0625 to 0.0625
- adapter_up_weight: bfloat16 [2048, 2048], P('ad', 'tp'), may hold values from -0.75 to 0.75
Outputs:
- kv_out: bfloat16 [2048, 2048], P('ad', 'tp')
Inputs may be any that keep to these rules, and one draw needn't show every extreme that they name: `request_group`: among the 256 rows of one index of ad, no group is named by more than 64 rows, a bound that some block reaches.
All inputs are finite; a program needn't handle non-finite values.
Results may differ from a plain program's by a relative error of at most 0.007.
Values may be sent and summed in bfloat16 or wider, within the bound.
No kernel may reach another device: no remote copies, remote signals or barrier semaphores. Data moves between devices by JAX's collectives and lax.ppermute only.
A program may use at most 128 MiB of HBM per device.

v0:
```python
import jax
import jax.numpy as jnp
from jax import lax
from jax.sharding import PartitionSpec as P

ADAPTER_RANK = 64


def shards(
    hidden, key_value_weight, request_group, request_member, adapter_down_weight, adapter_up_weight
):
    column_portion = adapter_down_weight.shape[0]
    adapter_pool_count = adapter_down_weight.shape[1] // ADAPTER_RANK
    base_output = jnp.dot(hidden, key_value_weight, preferred_element_type=jnp.float32)
    own_cols = lax.dynamic_slice_in_dim(
        hidden, lax.axis_index("tp") * column_portion, column_portion, 1
    )
    owner_index = request_group[:, 0]
    adapter = owner_index * adapter_pool_count + request_member
    block_portion = lax.all_gather(adapter_down_weight, "ad", axis=1, tiled=True)
    column_total = block_portion.shape[1]
    scores = jnp.dot(own_cols, block_portion, preferred_element_type=jnp.float32)
    column = jnp.arange(column_total, dtype=jnp.int32)
    kept_mask = (column // ADAPTER_RANK)[None, :] == adapter[:, None]
    selector = (
        (column % ADAPTER_RANK)[:, None] == jnp.arange(ADAPTER_RANK, dtype=jnp.int32)[None, :]
    ).astype(jnp.float32)
    partial_ranks = jnp.dot(
        jnp.where(kept_mask, scores, 0.0), selector, precision=lax.Precision.HIGHEST
    )
    rank_values = lax.psum(partial_ranks, "tp").astype(jnp.bfloat16)
    block_portion = lax.all_gather(adapter_up_weight, "ad", axis=0, tiled=True)
    line_total = block_portion.shape[0]
    row_index = jnp.arange(line_total, dtype=jnp.int32)
    spread = (
        (row_index % ADAPTER_RANK)[None, :] == jnp.arange(ADAPTER_RANK, dtype=jnp.int32)[:, None]
    ).astype(jnp.bfloat16)
    widened = jnp.dot(rank_values, spread, preferred_element_type=jnp.float32)
    kept_mask = (row_index // ADAPTER_RANK)[None, :] == adapter[:, None]
    raised_output = jnp.where(kept_mask, widened, 0.0).astype(jnp.bfloat16)
    adapter_update = jnp.dot(
        raised_output, block_portion, preferred_element_type=jnp.float32
    ).astype(jnp.bfloat16)
    return (base_output + adapter_update.astype(jnp.float32)).astype(jnp.bfloat16)


def solution(mesh):
    placed = (P("ad", None), P(None, "tp"), P("ad", None), P("ad"), P("tp", "ad"), P("ad", "tp"))
    return jax.shard_map(
        shards, mesh=mesh, in_specs=placed, out_specs=P("ad", "tp"), check_vma=False
    )
```

profile of v0, /device:TPU:0, one launch (start us, length us, event | category | flops | bytes accessed | tf_op | source)
XLA Modules:
  0.0 203.6 jit_solution(13971514790394120517)
XLA Ops:
  6.5 0.0 all-gather.3.cloned.1.call-start
  6.5 0.7 all-gather.3.cloned.1.call-update
  7.3 0.0 all-gather.5.cloned.1.call-start
  7.3 0.7 all-gather.5.cloned.1.call-update
  8.0 0.7 broadcast_multiply_fusion
  8.7 0.7 add.34
  9.4 127.7 %all-gather.3.cloned.1.call-done = bf16[2048,2048]{1,0:T(8,128)(2,1)} async-done(((bf16[2048,256]{1,0:T(8,128)(2,1)}), bf16[2048,2048]{1,0:T(8,128)(2,1)}) %all-gather.3.cloned.1.call-update) | async-done | bytes 8388624 | tf_op jit(solution)/shard_map/all_gather | solution.py:20
  137.1 6.1 %compare_select_fusion = f32[256,2048]{1,0:T(8,128)S(1)} fusion(bf16[2048,2048]{1,0:T(8,128)(2,1)} %all-gather.3.cloned.1.call-done, bf16[256,8192]{1,0:T(8,128)(2,1)} %param.6, s32[]{:T(128)S(6)} %select_n.40, s32[2048]{0:T(1024)S(1)} %get-tuple-element.6, s32[256]{0:T(256)S(1)} %add.34), kind=kOutput, calls=%fused_computation.1 | convolution fusion | flops 2148532224 | bytes 11543556 | tf_op jit(solution)/shard_map/dot_general | solution.py:22
  143.1 1.2 fusion.9
  144.4 12.5 %psum.7 = bf16[256,64]{1,0:T(8,128)(2,1)S(1)} all-reduce(f32[256,64]{1,0:T(8,128)S(1)} %fusion.9), channel_id=1, replica_groups=mesh['tp'=4,'ad'=8] {'tp'}, use_global_device_ids=true, to_apply=%region_0.1 | all-reduce | flops 16384 | bytes 98304 | tf_op jit(solution)/shard_map/psum | solution.py:31
  156.9 29.6 %all-gather.5.cloned.1.call-done = bf16[2048,512]{1,0:T(8,128)(2,1)} async-done(((bf16[256,512]{1,0:T(8,128)(2,1)}), bf16[2048,512]{1,0:T(8,128)(2,1)}) %all-gather.5.cloned.1.call-update) | async-done | bytes 2097168 | tf_op jit(solution)/shard_map/all_gather | solution.py:32
  186.5 2.6 %fusion.4 = f32[256,512]{1,0:T(8,128)S(1)} fusion(bf16[2048,512]{1,0:T(8,128)(2,1)} %all-gather.5.cloned.1.call-done, s32[2048]{0:T(1024)S(1)} %get-tuple-element.6, s32[256]{0:T(256)S(1)} %add.34, s32[2048]{0:T(1024)S(1)} %get-tuple-element.5, bf16[256,64]{1,0:T(8,128)(2,1)S(1)} %psum.7), kind=kOutput, calls=%fused_computation.7 | convolution fusion | flops 605945856 | bytes 2671616 | tf_op jit(solution)/shard_map/dot_general | solution.py:41
  189.1 7.7 %fusion.2 = bf16[256,512]{1,0:T(8,128)(2,1)} fusion(f32[256,512]{1,0:T(8,128)S(1)} %fusion.4, bf16[256,8192]{1,0:T(8,128)(2,1)} %param.6, bf16[8192,512]{1,0:T(8,128)(2,1)} %param.7), kind=kOutput, calls=%fused_computation.5 | convolution fusion | flops 2147745792 | bytes 13369344 | tf_op jit(solution)/shard_map/dot_general | solution.py:14
  (1 shorter events, 0.0 us)
Async XLA Ops:
  6.5 130.5 %all-gather.3.cloned.1.call-start = ((), (), s32[]{:S(2)}) async-start(), calls=%async_computation | async-start | bytes 9437184 | tf_op jit(solution)/shard_map/all_gather | solution.py:20
  7.3 179.2 %all-gather.5.cloned.1.call-start = ((), (), s32[]{:S(2)}) async-start(), calls=%async_computation.1 | async-start | bytes 2359296 | tf_op jit(solution)/shard_map/all_gather | solution.py:32
Sparse Core Ops, SparseCore 0:
  9.4 127.6 all-gather.2
  139.2 47.2 all-gather.4
where the time goes:
time: 204 us
  waiting for transfers between devices  159 us (78%)
  matrix products  17.5 us (9%)
  between operations  13.4 us (7%)
  blocking collectives  12.5 us (6%)
    all_gather x1, waiting for transfers between devices, shards(): lax.all_gather(adapter_down_weight, 'ad', axis=1, tiled=True)  128 us
    all_gather x1, waiting for transfers between devices, shards(): block_portion = lax.all_gather(adapter_up_weight, 'ad', axis=0, tiled=True)  29.6 us
    psum x1, blocking collectives, shards(): rank_values = lax.psum(partial_ranks, 'tp').astype(jnp.bfloat16)  12.5 us
    dot_general x1, matrix products, shards(): jnp.dot(hidden, key_value_weight, preferred_element_type=jnp.float32)  7.69 us
    dot_general x1, matrix products, shards(): jnp.dot(own_cols, block_portion, preferred_element_type=jnp.float32)  6.06 us
  transfers between devices with their start and end apart: 2, of which 2 were waited for; matrix products, arithmetic and copies ran while one was open for 4% of the time, Pallas kernels for 0%

commit v1 on v0

--- a/solution.py
+++ b/solution.py
@@ -17,7 +17,12 @@
     )
     owner_index = request_group[:, 0]
     adapter = owner_index * adapter_pool_count + request_member
-    block_portion = lax.all_gather(adapter_down_weight, "ad", axis=1, tiled=True)
+    ring = [adapter_down_weight]
+    for hop in range(7):
+        ring.append(lax.ppermute(ring[-1], "ad", [(dev, (dev + 1) % 8) for dev in range(8)]))
+    block_portion = jnp.roll(
+        jnp.concatenate(ring[::-1], axis=1), (lax.axis_index("ad") + 1) * ring[0].shape[1], axis=1
+    )
     column_total = block_portion.shape[1]
     scores = jnp.dot(own_cols, block_portion, preferred_element_type=jnp.float32)
     column = jnp.arange(column_total, dtype=jnp.int32)

time: 204 us -> 244 us (1.20)
  waiting for transfers between devices: 159 us -> 183 us
  local copies, waits for them, and re-layouts: 0 us -> 15.2 us
  starting transfers between devices: 0.04 us -> 2.98 us
    ppermute x0 -> x7, waiting for transfers between devices: none -> 183 us  [shards(): lax.ppermute(ring[-1], 'ad', [(dev, (dev + 1) % 8) for dev in range(8)])]
    all_gather x1 -> x0, waiting for transfers between devices: 128 us -> none  [shards(): lax.all_gather(adapter_down_weight, 'ad', axis=1, tiled=True)]
    all_gather x1, waiting for transfers between devices: 29.6 us -> 0.02 us  [shards(): block_portion = lax.all_gather(adapter_up_weight, 'ad', axis=0, tiled=True)]
    unnamed x0 -> x29, local copies, waits for them, and re-layouts: none -> 15.1 us
    ppermute x0 -> x7, starting transfers between devices: none -> 2.98 us  [shards(): lax.ppermute(ring[-1], 'ad', [(dev, (dev + 1) % 8) for dev in range(8)])]
  transfers between devices with their start and end apart: 2 -> 8, of which waited for: 2 -> 7; matrix products, arithmetic and copies ran while one was open for 4% -> 8% of each run, Pallas kernels for 0% -> 0%
where the time goes in v1:
time: 244 us
  waiting for transfers between devices  183 us (75%)
  local copies, waits for them, and re-layouts  15.2 us (6%)
  matrix products  15.1 us (6%)
  between operations  13.6 us (6%)
  blocking collectives  12.2 us (5%)
  starting transfers between devices  2.98 us (1%)
    ppermute x7, waiting for transfers between devices, shards(): lax.ppermute(ring[-1], 'ad', [(dev, (dev + 1) % 8) for dev in range(8)])  183 us
    unnamed x29, local copies, waits for them, and re-layouts  15.1 us
    psum x1, blocking collectives, shards(): rank_values = lax.psum(partial_ranks, 'tp').astype(jnp.bfloat16)  12.2 us
    dot_general x1, matrix products, shards(): jnp.dot(hidden, key_value_weight, preferred_element_type=jnp.float32)  7.69 us
  transfers between devices with their start and end apart: 8, of which 7 were waited for; matrix products, arithmetic and copies ran while one was open for 8% of the time, Pallas kernels for 0%

profile of v1, /device:TPU:0, one launch (start us, length us, event | category | flops | bytes accessed | tf_op | source)
XLA Modules:
  0.0 243.7 jit_solution(13255932322002448835)
XLA Ops:
  6.5 3.0 %collective-permute-start = (bf16[2048,256]{1,0:T(8,128)(2,1)}, bf16[2048,256]{1,0:T(8,128)(2,1)S(1)}, u32[]{:S(2)}, u32[]{:S(2)}) collective-permute-start(bf16[2048,256]{1,0:T(8,128)(2,1)} %param.10), channel_id=1, source_target_pairs={{0,1},{1,2},{2,3},{3,4},{4,5},{5,6},{6,7},{7,0},{8,9},{9,10},{10,1... | collective-permute-start | bytes 3145736 | tf_op jit(solution)/shard_map/ppermute | solution.py:22
  9.5 26.5 %collective-permute-done = bf16[2048,256]{1,0:T(8,128)(2,1)S(1)} collective-permute-done((bf16[2048,256]{1,0:T(8,128)(2,1)}, bf16[2048,256]{1,0:T(8,128)(2,1)S(1)}, u32[]{:S(2)}, u32[]{:S(2)}) %collective-permute-start) | collective-permute-done | bytes 1048608 | tf_op jit(solution)/shard_map/ppermute | solution.py:22
  36.0 27.0 %collective-permute-done.1 = bf16[2048,256]{1,0:T(8,128)(2,1)S(1)} collective-permute-done((bf16[2048,256]{1,0:T(8,128)(2,1)S(1)}, bf16[2048,256]{1,0:T(8,128)(2,1)S(1)}, u32[]{:S(2)}, u32[]{:S(2)}) %collective-permute-start.1) | collective-permute-done | bytes 1048608 | tf_op jit(solution)/shard_map/ppermute | solution.py:22
  63.0 26.2 %collective-permute-done.2 = bf16[2048,256]{1,0:T(8,128)(2,1)S(1)} collective-permute-done((bf16[2048,256]{1,0:T(8,128)(2,1)S(1)}, bf16[2048,256]{1,0:T(8,128)(2,1)S(1)}, u32[]{:S(2)}, u32[]{:S(2)}) %collective-permute-start.2) | collective-permute-done | bytes 1048608 | tf_op jit(solution)/shard_map/ppermute | solution.py:22
  89.2 1.0 copy-done.1
  90.1 25.3 %collective-permute-done.3 = bf16[2048,256]{1,0:T(8,128)(2,1)S(1)} collective-permute-done((bf16[2048,256]{1,0:T(8,128)(2,1)S(1)}, bf16[2048,256]{1,0:T(8,128)(2,1)S(1)}, u32[]{:S(2)}, u32[]{:S(2)}) %collective-permute-start.3) | collective-permute-done | bytes 1048608 | tf_op jit(solution)/shard_map/ppermute | solution.py:22
  115.4 1.0 copy-done.3
  116.4 24.4 %collective-permute-done.4 = bf16[2048,256]{1,0:T(8,128)(2,1)S(1)} collective-permute-done((bf16[2048,256]{1,0:T(8,128)(2,1)S(1)}, bf16[2048,256]{1,0:T(8,128)(2,1)S(1)}, u32[]{:S(2)}, u32[]{:S(2)}) %collective-permute-start.4) | collective-permute-done | bytes 1048608 | tf_op jit(solution)/shard_map/ppermute | solution.py:22
  140.9 1.0 copy-done.5
  141.9 23.7 %collective-permute-done.5 = bf16[2048,256]{1,0:T(8,128)(2,1)} collective-permute-done((bf16[2048,256]{1,0:T(8,128)(2,1)S(1)}, bf16[2048,256]{1,0:T(8,128)(2,1)}, u32[]{:S(2)}, u32[]{:S(2)}) %collective-permute-start.5) | collective-permute-done | bytes 1048608 | tf_op jit(solution)/shard_map/ppermute | solution.py:22
  165.6 0.8 broadcast_multiply_fusion
  166.5 0.8 add.47
  167.3 29.8 %collective-permute-done.6 = bf16[2048,256]{1,0:T(8,128)(2,1)} collective-permute-done((bf16[2048,256]{1,0:T(8,128)(2,1)}, bf16[2048,256]{1,0:T(8,128)(2,1)}, u32[]{:S(2)}, u32[]{:S(2)}) %collective-permute-start.6) | collective-permute-done | bytes 1048608 | tf_op jit(solution)/shard_map/ppermute | solution.py:22
  197.1 1.4 constant_dynamic-update-slice_fusion.15
  198.4 1.6 constant_dynamic-update-slice_fusion.14
  200.0 1.4 constant_dynamic-update-slice_fusion.13
  201.4 1.4 constant_dynamic-update-slice_fusion.12
  202.8 1.4 constant_dynamic-update-slice_fusion.11
  204.1 0.1 constant_dynamic-update-slice_fusion.10
  204.3 0.1 constant_dynamic-update-slice_fusion.9
  204.4 1.4 constant_dynamic-update-slice_fusion.8
  205.8 1.4 constant_dynamic-update-slice_fusion.7
  207.2 1.4 constant_dynamic-update-slice_fusion.6
  208.6 0.1 constant_dynamic-update-slice_fusion.5
  208.7 0.1 constant_dynamic-update-slice_fusion.4
  209.0 0.1 constant_dynamic-update-slice_fusion.2
  209.2 0.1 constant_dynamic-update-slice_fusion.1
  209.5 3.6 %compare_select_fusion = f32[256,2048]{1,0:T(8,128)S(1)} fusion(bf16[2048,4096]{1,0:T(8,128)(2,1)S(1)} %constant_dynamic-update-slice_fusion, s32[]{:T(128)S(6)} %select_n.54, bf16[256,8192]{1,0:T(8,128)(2,1)} %param.6, s32[]{:T(128)S(6)} %select_n.52, s32[2048]{0:T(1024)S(1)} %add_select_fusion, s32[256]{0:T(256)S(1)} %add.47), kind=kOutput, calls=%fused_computation.3 | convolution fusion | flops 2148532224 | bytes 11543560 | tf_op jit(solution)/shard_map/dot_general | solution.py:27
  213.1 1.2 fusion.13
  214.4 12.2 %psum.7 = bf16[256,64]{1,0:T(8,128)(2,1)S(1)} all-reduce(f32[256,64]{1,0:T(8,128)S(1)} %fusion.13), channel_id=1, replica_groups=mesh['tp'=4,'ad'=8] {'tp'}, use_global_device_ids=true, to_apply=%region_0.1 | all-reduce | flops 16384 | bytes 98304 | tf_op jit(solution)/shard_map/psum | solution.py:36
  226.6 2.6 %fusion.8 = f32[256,512]{1,0:T(8,128)S(1)} fusion(bf16[2048,512]{1,0:T(8,128)(2,1)} %all-gather.2.cloned.1.call-done, s32[2048]{0:T(1024)S(1)} %add_select_fusion, s32[256]{0:T(256)S(1)} %add.47, s32[2048]{0:T(1024)S(1)} %fusion.19, bf16[256,64]{1,0:T(8,128)(2,1)S(1)} %psum.7), kind=kOutput, calls=%fused_computation.9 | convolution fusion | flops 605945856 | bytes 2671616 | tf_op jit(solution)/shard_map/dot_general | solution.py:46
  229.1 7.7 %fusion.6 = bf16[256,512]{1,0:T(8,128)(2,1)} fusion(f32[256,512]{1,0:T(8,128)S(1)} %fusion.8, bf16[256,8192]{1,0:T(8,128)(2,1)} %param.6, bf16[8192,512]{1,0:T(8,128)(2,1)} %param.7), kind=kOutput, calls=%fused_computation.7 | convolution fusion | flops 2147745792 | bytes 13369344 | tf_op jit(solution)/shard_map/dot_general | solution.py:14
  (24 shorter events, 0.4 us)
Async XLA Ops:
  6.5 202.8 %copy-start = (bf16[2048,256]{1,0:T(8,128)(2,1)S(1)}, bf16[2048,256]{1,0:T(8,128)(2,1)}, u32[]{:S(2)}) copy-start(bf16[2048,256]{1,0:T(8,128)(2,1)} %param.10) | copy-start | bytes 3145732
  6.5 220.0 %all-gather.2.cloned.1.call-start = ((), (), s32[]{:S(2)}) async-start(), calls=%async_computation | async-start | bytes 2359296 | tf_op jit(solution)/shard_map/all_gather | solution.py:37
  6.5 29.4 %collective-permute-start = (bf16[2048,256]{1,0:T(8,128)(2,1)}, bf16[2048,256]{1,0:T(8,128)(2,1)S(1)}, u32[]{:S(2)}, u32[]{:S(2)}) collective-permute-start(bf16[2048,256]{1,0:T(8,128)(2,1)} %param.10), channel_id=1, source_target_pairs={{0,1},{1,2},{2,3},{3,4},{4,5},{5,6},{6,7},{7,0},{8,9},{9,10},{10,1... | collective-permute-start | bytes 3145736 | tf_op jit(solution)/shard_map/ppermute | solution.py:22
  36.0 27.0 %collective-permute-start.1 = (bf16[2048,256]{1,0:T(8,128)(2,1)S(1)}, bf16[2048,256]{1,0:T(8,128)(2,1)S(1)}, u32[]{:S(2)}, u32[]{:S(2)}) collective-permute-start(bf16[2048,256]{1,0:T(8,128)(2,1)S(1)} %collective-permute-done), channel_id=1, source_target_pairs={{0,1},{1,2},{2,3},{3,4},{4,5},{5,6},{6,7},{7,0},{8,9},{9,10},{10,1... | collective-permute-start | bytes 3145736 | tf_op jit(solution)/shard_map/ppermute | solution.py:22
  63.0 26.2 %collective-permute-start.2 = (bf16[2048,256]{1,0:T(8,128)(2,1)S(1)}, bf16[2048,256]{1,0:T(8,128)(2,1)S(1)}, u32[]{:S(2)}, u32[]{:S(2)}) collective-permute-start(bf16[2048,256]{1,0:T(8,128)(2,1)S(1)} %collective-permute-done.1), channel_id=1, source_target_pairs={{0,1},{1,2},{2,3},{3,4},{4,5},{5,6},{6,7},{7,0},{8,9},{9,10},{10,1... | collective-permute-start | bytes 3145736 | tf_op jit(solution)/shard_map/ppermute | solution.py:22
  89.2 1.0 copy-start.1
  90.1 25.3 %collective-permute-start.3 = (bf16[2048,256]{1,0:T(8,128)(2,1)S(1)}, bf16[2048,256]{1,0:T(8,128)(2,1)S(1)}, u32[]{:S(2)}, u32[]{:S(2)}) collective-permute-start(bf16[2048,256]{1,0:T(8,128)(2,1)S(1)} %collective-permute-done.2), channel_id=1, source_target_pairs={{0,1},{1,2},{2,3},{3,4},{4,5},{5,6},{6,7},{7,0},{8,9},{9,10},{10,1... | collective-permute-start | bytes 3145736 | tf_op jit(solution)/shard_map/ppermute | solution.py:22
  115.4 1.0 copy-start.3
  116.4 24.5 %collective-permute-start.4 = (bf16[2048,256]{1,0:T(8,128)(2,1)S(1)}, bf16[2048,256]{1,0:T(8,128)(2,1)S(1)}, u32[]{:S(2)}, u32[]{:S(2)}) collective-permute-start(bf16[2048,256]{1,0:T(8,128)(2,1)S(1)} %collective-permute-done.3), channel_id=1, source_target_pairs={{0,1},{1,2},{2,3},{3,4},{4,5},{5,6},{6,7},{7,0},{8,9},{9,10},{10,1... | collective-permute-start | bytes 3145736 | tf_op jit(solution)/shard_map/ppermute | solution.py:22
  140.9 1.0 copy-start.5
  141.9 23.7 %collective-permute-start.5 = (bf16[2048,256]{1,0:T(8,128)(2,1)S(1)}, bf16[2048,256]{1,0:T(8,128)(2,1)}, u32[]{:S(2)}, u32[]{:S(2)}) collective-permute-start(bf16[2048,256]{1,0:T(8,128)(2,1)S(1)} %collective-permute-done.4), channel_id=1, source_target_pairs={{0,1},{1,2},{2,3},{3,4},{4,5},{5,6},{6,7},{7,0},{8,9},{9,10},{10,1... | collective-permute-start | bytes 3145736 | tf_op jit(solution)/shard_map/ppermute | solution.py:22
  165.6 31.5 %collective-permute-start.6 = (bf16[2048,256]{1,0:T(8,128)(2,1)}, bf16[2048,256]{1,0:T(8,128)(2,1)}, u32[]{:S(2)}, u32[]{:S(2)}) collective-permute-start(bf16[2048,256]{1,0:T(8,128)(2,1)} %collective-permute-done.5), channel_id=1, source_target_pairs={{0,1},{1,2},{2,3},{3,4},{4,5},{5,6},{6,7},{7,0},{8,9},{9,10},{10,1... | collective-permute-start | bytes 3145736 | tf_op jit(solution)/shard_map/ppermute | solution.py:22
  165.6 42.9 %copy-start.6 = (bf16[2048,256]{1,0:T(8,128)(2,1)S(1)}, bf16[2048,256]{1,0:T(8,128)(2,1)}, u32[]{:S(2)}) copy-start(bf16[2048,256]{1,0:T(8,128)(2,1)} %copy-done.5) | copy-start | bytes 3145732
  165.6 43.1 %copy-start.4 = (bf16[2048,256]{1,0:T(8,128)(2,1)S(1)}, bf16[2048,256]{1,0:T(8,128)(2,1)}, u32[]{:S(2)}) copy-start(bf16[2048,256]{1,0:T(8,128)(2,1)} %copy-done.3) | copy-start | bytes 3145732
  165.6 43.2 %copy-start.2 = (bf16[2048,256]{1,0:T(8,128)(2,1)S(1)}, bf16[2048,256]{1,0:T(8,128)(2,1)}, u32[]{:S(2)}) copy-start(bf16[2048,256]{1,0:T(8,128)(2,1)} %copy-done.1) | copy-start | bytes 3145732
Sparse Core Ops, SparseCore 0:
  165.7 55.8 all-gather.1
